TPU v7x, 32 devices: a whole 2x2x4 slice. The times are simulated.
32 devices in a mesh: ia: 2 (over x), ja: 16 (over z, y, core).
Axes of the slice: x: 2, y: 2, z: 4, core: 2. Of those that a mesh axis runs over, the one named last changes fastest.
Arguments:
- phase_space: float32 [6, 32768], P(None, 'ja'), may hold values from -8 to 8, as said below
- derivatives: float32 [6, 32768], P(None, 'ja'), may hold values from -4 to 4
- potential: float32 [32768], P('ja'), may hold values from -4.5 to -0.5
- weights: float32 [32768], P('ja'), may hold values from 0.2 to 5
- levels: int32 [32768], P('ja'), may hold values from 0 to 7
- phases: float32 [32768], P('ja'), may hold values from 0.25 to 1
- active_index: int32 [2, 4096], P('ia'), may hold values from 0 to 32767, as said below
- active_count: int32 [2], P('ia'), may hold values from 512 to 4096, as said below
Outputs:
- new_phase_space: float32 [6, 32768], P(None, 'ja')
- new_derivatives: float32 [6, 32768], P(None, 'ja')
- new_potential: float32 [32768], P('ja')
- totals: float32 [5], replicated
Inputs may be any that keep to these rules, and one draw needn't show every extreme that they name: `phase_space`: positions lie within the range and velocities likewise. `active_index`: all 8192 entries are distinct star indices; in row g only the first active_count[g] entries are active stars, the rest are to be ignored. `active_count`: one list holds exactly 4096 active stars and each other between 512 and 1536.
All inputs are finite; a program needn't handle non-finite values.
Results may differ from a plain program's by a relative error of at most 0.0003.
Values sent between devices are 32-bit elements; how exact they have to be, the bound alone decides.
No kernel may reach another device: no remote copies, remote signals or barrier semaphores. Data moves between devices by JAX's collectives and lax.ppermute only.
A program may use at most 64 MiB of HBM per device.

v0:
```python
import math
import jax
import jax.numpy as jnp
from jax import lax
from jax.sharding import PartitionSpec as P

SOFTEN = 0.01
STEP_MAX = 0.5


def elapsed(levels, phases):
    return STEP_MAX * jnp.exp2(-levels.astype(jnp.float32)) * phases


def predict(phase_rows, deriv_rows, since_last):
    position = phase_rows[0:3]
    velocity = phase_rows[3:6]
    accel = deriv_rows[0:3]
    jerk_rate = deriv_rows[3:6]
    moved = position + since_last * (
        velocity + since_last * (accel * 0.5 + since_last * jerk_rate / 6.0)
    )
    turned = velocity + since_last * (accel + since_last * jerk_rate * 0.5)
    return (moved, turned)


def pair_block(block_pos, block_vel, block_ids, source_pos, source_vel, source_mass, source_ids):
    separation = source_pos[:, None, :] - block_pos[:, :, None]
    relative = source_vel[:, None, :] - block_vel[:, :, None]
    radius_sq = jnp.sum(separation * separation, 0) + SOFTEN
    inverse = 1.0 / jnp.sqrt(radius_sq)
    weighted = jnp.where(
        source_ids[None, :] == block_ids[:, None], 0.0, source_mass[None, :] * inverse
    )
    cubed = weighted * inverse * inverse
    radial = 3.0 * jnp.sum(separation * relative, 0) / radius_sq
    accel = jnp.sum(cubed * separation, 2)
    jerk_rate = jnp.sum(cubed * (relative - radial * separation), 2)
    binding = -jnp.sum(weighted, 1)
    return (accel, jerk_rate, binding)


def field_on(
    target_pos, target_vel, target_ids, source_pos, source_vel, source_mass, source_ids, block_len
):
    row_count = target_pos.shape[1]
    block_len = math.gcd(row_count, block_len)
    block_count = row_count // block_len

    def per_block(pieces):
        return pair_block(
            pieces[0], pieces[1], pieces[2], source_pos, source_vel, source_mass, source_ids
        )

    pieces = (
        jnp.transpose(target_pos.reshape(3, block_count, block_len), (1, 0, 2)),
        jnp.transpose(target_vel.reshape(3, block_count, block_len), (1, 0, 2)),
        target_ids.reshape(block_count, block_len),
    )
    accel, jerk_rate, binding = lax.map(per_block, pieces)
    accel = jnp.transpose(accel, (1, 0, 2)).reshape(3, row_count)
    jerk_rate = jnp.transpose(jerk_rate, (1, 0, 2)).reshape(3, row_count)
    binding = binding.reshape(1, row_count)
    return jnp.concatenate([accel, jerk_rate, binding], 0)


def correct(old_rows, field_rows):
    step_size = old_rows[14]
    old_pos = old_rows[0:3]
    old_vel = old_rows[3:6]
    old_acc = old_rows[6:9]
    old_jerk = old_rows[9:12]
    new_acc = field_rows[0:3]
    new_jerk = field_rows[3:6]
    new_vel = (
        old_vel
        + step_size * 0.5 * (old_acc + new_acc)
        + step_size * step_size / 12.0 * (old_jerk - new_jerk)
    )
    new_pos = (
        old_pos
        + step_size * 0.5 * (old_vel + new_vel)
        + step_size * step_size / 12.0 * (old_acc - new_acc)
    )
    return jnp.concatenate([new_pos, new_vel, new_acc, new_jerk, field_rows[6:7]], 0)


def star_terms(position, velocity, binding, star_mass):
    kinetic = 0.5 * star_mass * jnp.sum(velocity * velocity, 0)
    depth = 0.5 * star_mass * binding
    spin = jnp.stack(
        [
            position[1] * velocity[2] - position[2] * velocity[1],
            position[2] * velocity[0] - position[0] * velocity[2],
            position[0] * velocity[1] - position[1] * velocity[0],
        ],
        0,
    )
    return jnp.concatenate([kinetic[None], depth[None], star_mass[None] * spin], 0)


def reduce_field(partial_value, active_ids, is_alive):
    field_rows = lax.psum(partial_value, "ja")
    start = jnp.int32(0)
    return (field_rows, jnp.where(is_alive, active_ids, -1), is_alive, start)


def place_rows(base_rows, gathered, gathered_ids, shard, shard_len):
    target_col = gathered_ids - shard * shard_len
    keep_rows = (gathered_ids >= 0) & (target_col >= 0) & (target_col < shard_len)
    target = jnp.where(keep_rows, target_col, shard_len)
    return base_rows.at[:, target].set(gathered, mode="drop")


def per_device(
    phase_space, derivatives, potential, weights, levels, phases, active_index, active_count
):
    shard_len = phase_space.shape[1]
    shard_size = lax.axis_size("ja")
    star_count = shard_len * shard_size
    shard = lax.axis_index("ja")
    slot_count = active_index.shape[1]
    star_mass = weights / star_count
    since_last = elapsed(levels, phases)
    moved, turned = predict(phase_space, derivatives, since_last)
    star_ids = shard * shard_len + jnp.arange(shard_len, dtype=jnp.int32)
    active_ids = active_index[0]
    is_alive = jnp.arange(slot_count, dtype=jnp.int32) < active_count[0]
    local_col = active_ids - shard * shard_len
    is_local = (local_col >= 0) & (local_col < shard_len)
    safe_col = jnp.clip(local_col, 0, shard_len - 1)
    state_rows = jnp.concatenate(
        [phase_space, derivatives, potential[None], star_mass[None], since_last[None]], 0
    )
    base_rows = jnp.concatenate([phase_space, derivatives, potential[None]], 0)
    picked = jnp.where(is_local[None, :], jnp.take(state_rows, safe_col, axis=1), 0.0)
    old_sums = jnp.sum(star_terms(phase_space[0:3], phase_space[3:6], potential, star_mass), 1)
    fetched, old_total = lax.psum((picked, old_sums), "ja")
    block_pos, block_vel = predict(fetched[0:6], fetched[6:12], fetched[14])
    partial_value = field_on(
        block_pos, block_vel, active_ids, moved, turned, star_mass, star_ids, 256
    )
    field_rows, share_ids, share_alive, start = reduce_field(partial_value, active_ids, is_alive)
    updated = correct(fetched, field_rows)
    change = star_terms(updated[0:3], updated[3:6], updated[12], fetched[13]) - star_terms(
        fetched[0:3], fetched[3:6], fetched[12], fetched[13]
    )
    payload = jnp.concatenate([updated, jnp.where(share_alive[None, :], change, 0.0)], 0)
    gathered, gathered_ids = (
        lax.all_gather(payload, "ia", axis=1, tiled=True),
        lax.all_gather(share_ids, "ia", axis=0, tiled=True),
    )
    new_state = place_rows(base_rows, gathered[0:13], gathered_ids, shard, shard_len)
    totals = old_total + jnp.sum(gathered[13:18], 1)
    return (new_state[0:6], new_state[6:12], new_state[12], totals)


def solution(mesh):
    placed = (
        P(None, "ja"),
        P(None, "ja"),
        P("ja"),
        P("ja"),
        P("ja"),
        P("ja"),
        P("ia", None),
        P("ia"),
    )
    return jax.shard_map(
        per_device,
        mesh=mesh,
        in_specs=placed,
        out_specs=(P(None, "ja"), P(None, "ja"), P("ja"), P()),
        check_vma=False,
    )
```

profile of v0, /device:TPU:0, one launch (start us, length us, event | category | flops | bytes accessed | tf_op | source)
XLA Modules:
  0.0 349.2 jit_solution(14010528817504141636)
XLA Ops:
  11.2 2.6 concatenate.23
  14.2 10.8 %gather_fusion = f32[4096,15]{1,0:T(8,128)S(1)} fusion(f32[15,2048]{0,1:T(8,128)S(1)} %copy.113, s32[4096]{0:T(1024)S(1)} %broadcast_clamp_fusion), kind=kCustom, calls=%fused_computation | custom fusion | bytes 507904 | tf_op jit(solution)/shard_map/jit(_take)/gather | solution.py:136
  28.5 5.3 %all_gather.6 = s32[8192]{0:T(1024)S(1)} all-gather(s32[4096]{0:T(1024)S(1)} %broadcast_select_fusion), channel_id=1, replica_groups=mesh['ia'=2,'ja'=16] {'ia'}, dimensions={0}, use_global_device_ids=true | all-gather | bytes 49152 | tf_op jit(solution)/shard_map/all_gather | solution.py:151
  34.3 32.9 %psum.23 = f32[5]{0:T(128)S(1)} all-reduce(f32[5]{0:T(128)S(1)} %maximum_reduce_fusion), channel_id=1, replica_groups=mesh['ia'=2,'ja'=16] {'ja'}, use_global_device_ids=true, to_apply=%region_14.15 | all-reduce | flops 5 | bytes 40 | tf_op jit(solution)/shard_map/psum | solution.py:138
  67.3 51.7 %all-reduce.3.cloned.1.call-done = f32[15,4096]{1,0:T(8,128)} async-done(((f32[15,4096]{1,0:T(8,128)}), f32[15,4096]{1,0:T(8,128)}) %all-reduce.3.cloned.1.call-update) | async-done | bytes 245776 | tf_op jit(solution)/shard_map/psum | solution.py:138
  121.3 85.2 %while.15 = (s32[]{:T(128)}, f32[16,3,256]{2,1,0:T(4,128)S(1)}, f32[16,3,256]{2,1,0:T(4,128)S(1)}, f32[16,256]{1,0:T(8,128)S(1)}, s32[16,256]{1,0:T(8,128)S(1)},...) while((s32[]{:T(128)}, f32[16,3,256]{2,1,0:T(4,128)S(1)}, ...), condition=%wide.region_7.8_spmd.clone, body=%wide.region_1.7_spmd.clone.sunk | while | flops 25690624 | bytes 16955540 | solution.py:60
  121.4 2.1 fusion.18
  124.4 2.2 fusion.20
  126.7 2.1 fusion.18
  129.7 2.2 fusion.20
  132.0 2.1 fusion.18
  135.0 2.2 fusion.20
  137.4 2.1 fusion.18
  140.4 2.2 fusion.20
  145.7 2.2 fusion.20
  148.0 2.1 fusion.18
  151.0 2.2 fusion.20
  156.3 2.2 fusion.20
  158.7 2.1 fusion.18
  161.7 2.2 fusion.20
  167.0 2.2 fusion.20
  172.3 2.2 fusion.20
  177.6 2.2 fusion.20
  183.0 2.2 fusion.20
  188.3 2.2 fusion.20
  193.6 2.2 fusion.20
  199.0 2.2 fusion.20
  204.3 2.2 fusion.20
  207.3 88.8 %all-reduce.5.cloned.1.call-done = f32[7,4096]{1,0:T(8,128)} async-done(((f32[7,4096]{1,0:T(8,128)}), f32[7,4096]{1,0:T(8,128)}) %all-reduce.5.cloned.1.call-update) | async-done | bytes 114704 | tf_op jit(solution)/shard_map/psum | solution.py:103
  300.6 11.8 %all_gather.7 = f32[18,8192]{1,0:T(8,128)S(1)} all-gather(f32[18,4096]{1,0:T(8,128)S(1)} %pad_maximum_fusion), channel_id=1, replica_groups=mesh['ia'=2,'ja'=16] {'ia'}, dimensions={1}, use_global_device_ids=true | all-gather | bytes 884736 | tf_op jit(solution)/shard_map/all_gather | solution.py:150
  313.3 2.6 copy.118
  315.9 21.2 %scatter_fusion = f32[13,2048]{0,1:T(8,128)S(1)} fusion(f32[13,2048]{0,1:T(8,128)S(1)} %copy.117, s32[8192]{0:T(1024)S(1)} %compare_select_fusion.1, f32[8192,13]{1,0:T(8,128)} %copy.118), kind=kCustom, calls=%fused_computation.1 | custom fusion | bytes 1310720 | tf_op jit(solution)/shard_map/scatter | solution.py:112
  (196 shorter events, 57.7 us)
Async XLA Ops:
  7.2 111.8 %all-reduce.3.cloned.1.call-start = ((), (), s32[]{:S(2)}) async-start(), calls=%async_computation | async-start | bytes 524288 | tf_op jit(solution)/shard_map/psum | solution.py:138
  14.1 11.5 %copy-start.4 = (s32[1,4096]{1,0:T(1,128)S(1)}, s32[1,4096]{1,0:T(1,128)}, u32[]{:S(2)}) copy-start(s32[1,4096]{1,0:T(1,128)} %param.16) | copy-start | bytes 49156
  24.9 1.5 copy-start.2
  25.0 1.5 copy-start.3
  25.0 1.5 copy-start.5
  26.4 269.7 %all-reduce.5.cloned.1.call-start = ((), (), s32[]{:S(2)}) async-start(), calls=%async_computation.1 | async-start | bytes 262144 | tf_op jit(solution)/shard_map/psum | solution.py:103
  121.3 174.8 %copy-start.1 = (f32[15,4096]{1,0:T(8,128)S(1)}, f32[15,4096]{1,0:T(8,128)}, u32[]{:S(2)}) copy-start(f32[15,4096]{1,0:T(8,128)} %all-reduce.3.cloned.1.call-done) | copy-start | bytes 737284
  312.4 0.9 copy-start
Sparse Core Ops, SparseCore 0:
  26.5 92.4 all-reduce.2
  207.4 88.6 all-reduce.4
where the time goes:
time: 350 us; the launch traced here: 349 us
  waiting for transfers between devices  141 us (40%)
  other arithmetic  97.5 us (28%)
  blocking collectives  50 us (14%)
  local copies, waits for them, and re-layouts  44.9 us (13%)
  between operations  14.9 us (4%)
    psum x1, waiting for transfers between devices, reduce_field(): field_rows = lax.psum(partial_value, 'ja')  88.8 us
    psum x1, waiting for transfers between devices, per_device(): fetched, old_total = lax.psum((picked, old_sums), 'ja')  51.7 us
    reduce_sum x16, other arithmetic, pair_block(): jerk_rate = jnp.sum(cubed * (relative - radial * separation), 2)  35.1 us
    reduce_sum x16, other arithmetic, pair_block(): radial = 3.0 * jnp.sum(separation * relative, 0) / radius_sq  33.4 us
    psum x1, blocking collectives, per_device(): fetched, old_total = lax.psum((picked, old_sums), 'ja')  32.9 us
    scatter x1, local copies, waits for them, and re-layouts, place_rows(): return base_rows.at[:, target].set(gathered, mode='drop')  21.2 us
    reduce_sum x16, other arithmetic, pair_block(): binding = -jnp.sum(weighted, 1)  14 us
    all_gather x1, blocking collectives, per_device(): lax.all_gather(payload, 'ia', axis=1, tiled=True)  11.8 us
  transfers between devices with their start and end apart: 2, of which 2 were waited for; matrix products, arithmetic and copies ran while one was open for 1% of the time, Pallas kernels for 0%

commit v1 on v0

--- a/solution.py
+++ b/solution.py
@@ -6,6 +6,12 @@
 
 SOFTEN = 0.01
 STEP_MAX = 0.5
+
+
+def gather_and_add(array, name):
+    parts = lax.all_gather(array, name, axis=0, tiled=False)
+    acc = parts.sum(axis=0)
+    return acc
 
 
 def elapsed(levels, phases):
@@ -100,7 +106,7 @@
 
 
 def reduce_field(partial_value, active_ids, is_alive):
-    field_rows = lax.psum(partial_value, "ja")
+    field_rows = gather_and_add(partial_value, "ja")
     start = jnp.int32(0)
     return (field_rows, jnp.where(is_alive, active_ids, -1), is_alive, start)
 

time: 350 us -> 301 us (0.86)
  waiting for transfers between devices: 141 us -> 95.5 us
    psum x1 -> x0, waiting for transfers between devices: 88.8 us -> none  [reduce_field(): field_rows = lax.psum(partial_value, 'ja')]
    psum x1, waiting for transfers between devices: 51.7 us -> 91.3 us  [per_device(): fetched, old_total = lax.psum((picked, old_sums), 'ja')]
    all_gather x0 -> x1, waiting for transfers between devices: none -> 4.22 us  [gather_and_add(): parts = lax.all_gather(array, name, axis=0, tiled=False)]
where the time goes in v1:
time: 301 us
  other arithmetic  95.5 us (32%)
  waiting for transfers between devices  95.5 us (32%)
  blocking collectives  48.5 us (16%)
  local copies, waits for them, and re-layouts  44.9 us (15%)
  between operations  15 us (5%)
    psum x1, waiting for transfers between devices, per_device(): fetched, old_total = lax.psum((picked, old_sums), 'ja')  91.3 us
    reduce_sum x16, other arithmetic, pair_block(): jerk_rate = jnp.sum(cubed * (relative - radial * separation), 2)  35.1 us
    reduce_sum x16, other arithmetic, pair_block(): radial = 3.0 * jnp.sum(separation * relative, 0) / radius_sq  33.4 us
    psum x1, blocking collectives, per_device(): fetched, old_total = lax.psum((picked, old_sums), 'ja')  32.2 us
    scatter x1, local copies, waits for them, and re-layouts, place_rows(): return base_rows.at[:, target].set(gathered, mode='drop')  21.2 us
    reduce_sum x16, other arithmetic, pair_block(): binding = -jnp.sum(weighted, 1)  14 us
    all_gather x1, blocking collectives, per_device(): lax.all_gather(payload, 'ia', axis=1, tiled=True)  11.9 us
    gather x2, local copies, waits for them, and re-layouts, per_device(): jnp.take(state_rows, safe_col, axis=1)  11.4 us
  transfers between devices with their start and end apart: 2, of which 2 were waited for; matrix products, arithmetic and copies ran while one was open for 1% of the time, Pallas kernels for 0%

profile of v1, /device:TPU:0, one launch (start us, length us, event | category | flops | bytes accessed | tf_op | source)
XLA Modules:
  0.0 300.7 jit_solution(8879476847903044437)
XLA Ops:
  11.2 2.6 concatenate.23
  14.2 10.8 %gather_fusion = f32[4096,15]{1,0:T(8,128)S(1)} fusion(f32[15,2048]{0,1:T(8,128)S(1)} %copy.144, s32[4096]{0:T(1024)S(1)} %broadcast_clamp_fusion), kind=kCustom, calls=%fused_computation | custom fusion | bytes 507904 | tf_op jit(solution)/shard_map/jit(_take)/gather | solution.py:142
  27.7 91.3 %all-reduce.2.cloned.1.call-done = f32[15,4096]{1,0:T(8,128)} async-done(((f32[15,4096]{1,0:T(8,128)}), f32[15,4096]{1,0:T(8,128)}) %all-reduce.2.cloned.1.call-update) | async-done | bytes 245776 | tf_op jit(solution)/shard_map/psum | solution.py:144
  121.3 85.2 %while.15 = (s32[]{:T(128)}, f32[16,3,256]{2,1,0:T(4,128)S(1)}, f32[16,3,256]{2,1,0:T(4,128)S(1)}, f32[16,256]{1,0:T(8,128)S(1)}, s32[16,256]{1,0:T(8,128)S(1)},...) while((s32[]{:T(128)}, f32[16,3,256]{2,1,0:T(4,128)S(1)}, ...), condition=%wide.region_7.8_spmd.clone, body=%wide.region_1.7_spmd.clone.sunk | while | flops 25690624 | bytes 16955540 | solution.py:66
  121.3 2.1 fusion.18
  124.3 2.2 fusion.20
  126.6 2.1 fusion.18
  129.6 2.2 fusion.20
  135.0 2.2 fusion.20
  137.3 2.1 fusion.18
  140.3 2.2 fusion.20
  145.6 2.2 fusion.20
  148.0 2.1 fusion.18
  151.0 2.2 fusion.20
  153.3 2.1 fusion.18
  156.3 2.2 fusion.20
  158.6 2.1 fusion.18
  161.6 2.2 fusion.20
  166.9 2.2 fusion.20
  172.3 2.2 fusion.20
  177.6 2.2 fusion.20
  182.9 2.2 fusion.20
  188.2 2.2 fusion.20
  193.6 2.2 fusion.20
  198.9 2.2 fusion.20
  204.2 2.2 fusion.20
  207.5 32.2 %psum.15 = f32[5]{0:T(128)S(1)} all-reduce(f32[5]{0:T(128)S(1)} %maximum_reduce_fusion), channel_id=1, replica_groups=mesh['ia'=2,'ja'=16] {'ja'}, use_global_device_ids=true, to_apply=%region_14.15 | all-reduce | flops 5 | bytes 40 | tf_op jit(solution)/shard_map/psum | solution.py:144
  240.8 4.4 %all_gather.12 = s32[8192]{0:T(1024)S(1)} all-gather(s32[4096]{0:T(1024)S(1)} %broadcast_select_fusion), channel_id=1, replica_groups=mesh['ia'=2,'ja'=16] {'ia'}, dimensions={0}, use_global_device_ids=true | all-gather | bytes 49152 | tf_op jit(solution)/shard_map/all_gather | solution.py:157
  245.2 4.2 %all-gather.4.cloned.1.call-done = f32[16,7,4096]{2,1,0:T(8,128)} async-done(((f32[1,7,4096]{2,1,0:T(8,128)}), f32[16,7,4096]{2,1,0:T(8,128)}) %all-gather.4.cloned.1.call-update) | async-done | bytes 1835024 | tf_op jit(solution)/shard_map/all_gather | solution.py:12
  251.9 11.9 %all_gather.15 = f32[18,8192]{1,0:T(8,128)S(1)} all-gather(f32[18,4096]{1,0:T(8,128)S(1)} %pad_maximum_fusion), channel_id=1, replica_groups=mesh['ia'=2,'ja'=16] {'ia'}, dimensions={1}, use_global_device_ids=true | all-gather | bytes 884736 | tf_op jit(solution)/shard_map/all_gather | solution.py:156
  264.8 2.6 copy.149
  267.4 21.2 %scatter_fusion = f32[13,2048]{0,1:T(8,128)S(1)} fusion(f32[13,2048]{0,1:T(8,128)S(1)} %copy.148, s32[8192]{0:T(1024)S(1)} %compare_select_fusion.1, f32[8192,13]{1,0:T(8,128)} %copy.149), kind=kCustom, calls=%fused_computation.1 | custom fusion | bytes 1310720 | tf_op jit(solution)/shard_map/scatter | solution.py:118
  (197 shorter events, 55.7 us)
Async XLA Ops:
  7.2 111.8 %all-reduce.2.cloned.1.call-start = ((), (), s32[]{:S(2)}) async-start(), calls=%async_computation | async-start | bytes 524288 | tf_op jit(solution)/shard_map/psum | solution.py:144
  14.1 11.4 %copy-start.4 = (s32[1,4096]{1,0:T(1,128)S(1)}, s32[1,4096]{1,0:T(1,128)}, u32[]{:S(2)}) copy-start(s32[1,4096]{1,0:T(1,128)} %param.16) | copy-start | bytes 49156
  26.4 223.1 %all-gather.4.cloned.1.call-start = ((), (), s32[]{:S(2)}) async-start(), calls=%async_computation.1 | async-start | bytes 2228224 | tf_op jit(solution)/shard_map/all_gather | solution.py:12
  121.2 86.0 %copy-start.2 = (f32[6,2048]{1,0:T(8,128)S(1)}, f32[6,2048]{1,0:T(8,128)}, u32[]{:S(2)}) copy-start(f32[6,2048]{1,0:T(8,128)} %param.10) | copy-start | bytes 147460
  121.2 119.1 %copy-start.3 = (f32[6,2048]{1,0:T(8,128)S(1)}, f32[6,2048]{1,0:T(8,128)}, u32[]{:S(2)}) copy-start(f32[6,2048]{1,0:T(8,128)} %param.11) | copy-start | bytes 147460
  121.3 119.1 %copy-start.5 = (f32[2048]{0:T(1024)S(1)}, f32[2048]{0:T(1024)}, u32[]{:S(2)}) copy-start(f32[2048]{0:T(1024)} %param.12) | copy-start | bytes 24580
  207.2 44.0 %copy-start.1 = (f32[15,4096]{1,0:T(8,128)S(1)}, f32[15,4096]{1,0:T(8,128)}, u32[]{:S(2)}) copy-start(f32[15,4096]{1,0:T(8,128)} %all-reduce.2.cloned.1.call-done) | copy-start | bytes 737284
  263.9 0.9 copy-start
Sparse Core Ops, SparseCore 0:
  26.5 92.4 all-reduce.1
  207.4 42.0 all-gather.3
